TPU v7x, 256 devices: a whole 4x4x8 slice. The times are simulated.
256 devices in a mesh: blk: 64 (over z, x, core), rep: 4 (over y).
Axes of the slice: x: 4, y: 4, z: 8, core: 2. Of those that a mesh axis runs over, the one named last changes fastest.
Arguments:
- amplitudes: float32 [64, 64, 16, 512], P('blk', None, 'rep'), may hold values from -6 to 6
- cycle_integrals: float32 [32, 64, 64, 512], P('rep', None, 'blk'), may hold values from -0.09375 to 0.09375
- cross_integrals: float32 [32, 64, 64, 512], P('rep', None, 'blk'), may hold values from -0.09375 to 0.09375
- occ_energy: float32 [64], replicated, may hold values from -2 to -0.5
- vir_energy_a: float32 [32], replicated, may hold values from 0.2 to 3
- vir_energy_b: float32 [16], replicated, may hold values from 0.2 to 3
Outputs:
- update: float32 [64, 32, 16, 64], P('blk', 'rep')
- residual_rms: float32 [], replicated
All inputs are finite; a program needn't handle non-finite values.
Results may differ from a plain program's by a relative error of at most 0.0006.
Values sent between devices are 32-bit elements; how exact they have to be, the bound alone decides.
A program may use at most 64 MiB of HBM per device.

v0:
```python
import jax
import jax.numpy as jnp
from jax import lax
from jax.sharding import PartitionSpec as P


def per_device(
    amplitudes, cycle_integrals, cross_integrals, occ_energy, vir_energy_a, vir_energy_b
):
    highest = lax.Precision.HIGHEST
    whole = lax.all_gather(amplitudes, "rep", axis=2, tiled=True)
    moved = lax.all_to_all(whole, "blk", split_axis=1, concat_axis=0, tiled=True)
    crossed = jnp.swapaxes(moved, 0, 1)
    rows = amplitudes.shape[0]
    part = cycle_integrals
    cycle = lax.psum_scatter(
        jnp.einsum("aikc,kjbc->iabj", part, whole, precision=highest),
        "blk",
        scatter_dimension=0,
        tiled=True,
    )
    part = cross_integrals
    cross = lax.psum_scatter(
        jnp.einsum("aikc,kjbc->iabj", part, crossed, precision=highest),
        "blk",
        scatter_dimension=0,
        tiled=True,
    )
    residual = cycle + cross
    a_count = cycle_integrals.shape[0]
    occ_local = lax.dynamic_slice_in_dim(occ_energy, lax.axis_index("blk") * rows, rows, 0)
    vir_local = lax.dynamic_slice_in_dim(vir_energy_a, lax.axis_index("rep") * a_count, a_count, 0)
    denom = (
        occ_local[:, None, None, None]
        + occ_energy[None, None, None, :]
        - vir_local[None, :, None, None]
        - vir_energy_b[None, None, :, None]
    )
    update = residual / denom
    squares = lax.psum(jnp.sum(residual * residual), ("blk", "rep"))
    total_count = (
        occ_energy.shape[0] * occ_energy.shape[0] * vir_energy_a.shape[0] * vir_energy_b.shape[0]
    )
    residual_rms = jnp.sqrt(squares / total_count)
    return (update, residual_rms)


def solution(mesh):
    return jax.shard_map(
        per_device,
        mesh=mesh,
        in_specs=(
            P("blk", None, "rep", None),
            P("rep", None, "blk", None),
            P("rep", None, "blk", None),
            P(),
            P(),
            P(),
        ),
        out_specs=(P("blk", "rep", None, None), P()),
        check_vma=False,
    )
```

profile of v0, /device:TPU:1, one launch (start us, length us, event | category | flops | bytes accessed | tf_op | source)
XLA Modules:
  0.0 354.6 jit_solution(3494779001392865081)
XLA Ops:
  7.2 0.0 all-gather.2.cloned.1.call-start
  7.2 2.0 copy.9
  9.2 0.0 all-gather.2.cloned.1.call-update
  9.2 37.5 %all-gather.2.cloned.1.call-done = f32[1,64,16,512]{3,1,0,2:T(8,128)} async-done(((f32[1,64,4,512]{3,1,0,2:T(8,128)}), f32[1,64,16,512]{3,1,0,2:T(8,128)}) %all-gather.2.cloned.1.call-update) | async-done | bytes 2097168 | tf_op jit(solution)/shard_map/all_gather | solution.py:11
  46.8 4.2 %copy.11 = f32[1,64,16,512]{3,2,0,1:T(8,128)} copy(f32[1,64,16,512]{3,1,0,2:T(8,128)} %all-gather.2.cloned.1.call-done) | data formatting | bytes 4194304 | tf_op jit(solution)/shard_map/all_gather | solution.py:11
  50.9 0.0 copy-start
  50.9 0.0 copy-start.1
  50.9 11.3 %all-to-all-start = ((f32[1,64,16,512]{3,2,0,1:T(8,128)}), f32[1,64,16,512]{3,2,0,1:T(8,128)}, u32[]{:S(2)}, u32[]{:S(2)}) async-start(f32[1,64,16,512]{3,2,0,1:T(8,128)} %copy.11), calls=%async_computation | async-start | bytes 4194304 | tf_op jit(solution)/shard_map/all_to_all | solution.py:12
  62.2 0.0 reduce-scatter.4.cloned.1.call-start
  62.3 0.0 copy-done
  62.3 0.0 copy-done.1
  62.3 9.0 %fusion.1 = f32[64,16,8,64]{3,1,2,0:T(8,128)} fusion(f32[1,64,16,512]{3,1,0,2:T(8,128)S(1)} %copy-done, f32[8,64,1,512]{3,2,1,0:T(1,128)S(1)} %copy-done.1), kind=kOutput, calls=%fused_computation.2 | convolution fusion | flops 3221225472 | bytes 5242880 | tf_op jit(solution)/shard_map/aikc,kjbc->iabj/dot_general | solution.py:17
  71.3 40.6 %all-to-all-done = f32[1,64,16,512]{3,2,0,1:T(8,128)} async-done(((f32[1,64,16,512]{3,2,0,1:T(8,128)}), f32[1,64,16,512]{3,2,0,1:T(8,128)}, u32[]{:S(2)}, u32[]{:S(2)}) %all-to-all-start) | async-done | bytes 2097184 | tf_op jit(solution)/shard_map/all_to_all | solution.py:12
  111.9 10.5 %add_bitcast_fusion = f32[64,8,16,64]{0,2,1,3:T(8,128)} fusion(f32[64,16,8,64]{3,1,2,0:T(8,128)} %fusion.1, f32[1,64,16,512]{3,2,0,1:T(8,128)} %all-to-all-done, f32[8,64,1,512]{3,2,1,0:T(1,128)} %param.8), kind=kOutput, calls=%fused_computation | convolution fusion | flops 3221749760 | bytes 7340032 | tf_op jit(solution)/shard_map/aikc,kjbc->iabj/dot_general | solution.py:24
  122.4 6.1 %copy.12 = f32[64,8,16,64]{3,2,1,0:T(8,128)} copy(f32[64,8,16,64]{0,2,1,3:T(8,128)} %add_bitcast_fusion) | data formatting | bytes 4194304 | tf_op jit(solution)/shard_map/add | solution.py:29
  128.5 0.0 copy-start.4
  128.5 0.0 copy-start.3
  128.5 0.0 copy-start.2
  128.5 0.0 reduce-scatter.4.cloned.1.call-update
  128.5 0.6 copy-done.4
  129.1 0.6 dynamic_slice.6
  129.7 0.0 copy-done.3
  129.7 0.1 dynamic_slice.7
  129.8 0.6 broadcast_add_fusion
  130.4 0.1 broadcast_subtract_fusion
  130.5 133.6 %reduce-scatter.4.cloned.1.call-done = f32[1,8,16,64]{3,2,1,0:T(8,128)} async-done(((f32[64,8,16,64]{3,2,1,0:T(8,128)}), f32[1,8,16,64]{3,2,1,0:T(8,128)}) %reduce-scatter.4.cloned.1.call-update) | async-done | bytes 32784
  264.1 0.0 copy-done.2
  264.1 2.1 multiply_reduce_fusion
  266.2 79.7 %psum.7 = f32[]{:T(128)} all-reduce(f32[]{:T(128)} %get-tuple-element.4), channel_id=1, replica_groups=mesh['blk'=64,'rep'=4] {'blk','rep'}, use_global_device_ids=true, to_apply=%region_3.0 | all-reduce | flops 1 | bytes 8 | tf_op jit(solution)/shard_map/psum | solution.py:40
Async XLA Ops:
  7.2 39.6 %all-gather.2.cloned.1.call-start = ((), (), s32[]{:S(2)}) async-start(), calls=%async_computation.2 | async-start | bytes 2621440 | tf_op jit(solution)/shard_map/all_gather | solution.py:11
  50.9 11.3 %copy-start = (f32[1,64,16,512]{3,1,0,2:T(8,128)S(1)}, f32[1,64,16,512]{3,1,0,2:T(8,128)}, u32[]{:S(2)}) copy-start(f32[1,64,16,512]{3,1,0,2:T(8,128)} %all-gather.2.cloned.1.call-done) | copy-start | bytes 6291460
  50.9 11.3 %copy-start.1 = (f32[8,64,1,512]{3,2,1,0:T(1,128)S(1)}, f32[8,64,1,512]{3,2,1,0:T(1,128)}, u32[]{:S(2)}) copy-start(f32[8,64,1,512]{3,2,1,0:T(1,128)} %param.7) | copy-start | bytes 3145732
  50.9 60.9 %all-to-all-start = ((f32[1,64,16,512]{3,2,0,1:T(8,128)}), f32[1,64,16,512]{3,2,0,1:T(8,128)}, u32[]{:S(2)}, u32[]{:S(2)}) async-start(f32[1,64,16,512]{3,2,0,1:T(8,128)} %copy.11), calls=%async_computation | async-start | bytes 4194304 | tf_op jit(solution)/shard_map/all_to_all | solution.py:12
  62.2 201.9 %reduce-scatter.4.cloned.1.call-start = ((), (), s32[]{:S(2)}) async-start(), calls=%async_computation.3 | async-start | bytes 4259840
  128.5 0.7 copy-start.4
  128.5 1.2 copy-start.3
  128.5 135.6 %copy-start.2 = (f32[16]{0:T(128)S(1)}, f32[16]{0:T(128)}, u32[]{:S(2)}) copy-start(f32[16]{0:T(128)} %param.11) | copy-start | bytes 196
Sparse Core Ops, SparseCore 0:
  9.8 36.9 all-gather.1
  128.6 135.4 reduce-scatter.3
where the time goes:
time: 355 us
  waiting for transfers between devices  212 us (60%)
  blocking collectives  79.7 us (22%)
  matrix products  19.5 us (5%)
  between operations  15.9 us (4%)
  local copies, waits for them, and re-layouts  13.5 us (4%)
  starting transfers between devices  11.4 us (3%)
    unnamed x3, waiting for transfers between devices  134 us
    psum x1, blocking collectives, per_device(): squares = lax.psum(jnp.sum(residual * residual), ('blk', 'rep'))  79.7 us
    all_to_all x1, waiting for transfers between devices, per_device(): lax.all_to_all(whole, 'blk', split_axis=1, concat_axis=0, tiled=True)  40.6 us
    all_gather x1, waiting for transfers between devices, per_device(): whole = lax.all_gather(amplitudes, 'rep', axis=2, tiled=True)  37.5 us
    all_to_all x1, starting transfers between devices, per_device(): lax.all_to_all(whole, 'blk', split_axis=1, concat_axis=0, tiled=True)  11.3 us
    dot_general x1, matrix products, per_device(): jnp.einsum('aikc,kjbc->iabj', part, crossed, precision=highest)  10.5 us
    dot_general x1, matrix products, per_device(): jnp.einsum('aikc,kjbc->iabj', part, whole, precision=highest)  8.97 us
  transfers between devices with their start and end apart: 3, of which 3 were waited for; matrix products, arithmetic and copies ran while one was open for 3% of the time, Pallas kernels for 0%

commit v1 on v0

--- a/solution.py
+++ b/solution.py
@@ -8,7 +8,10 @@
     amplitudes, cycle_integrals, cross_integrals, occ_energy, vir_energy_a, vir_energy_b
 ):
     highest = lax.Precision.HIGHEST
-    whole = lax.all_gather(amplitudes, "rep", axis=2, tiled=True)
+    size = lax.axis_size("rep")
+    blocks = jnp.stack([amplitudes for _ in range(size)])
+    blocks = lax.all_to_all(blocks, "rep", split_axis=0, concat_axis=0)
+    whole = jnp.concatenate(blocks, axis=2)
     moved = lax.all_to_all(whole, "blk", split_axis=1, concat_axis=0, tiled=True)
     crossed = jnp.swapaxes(moved, 0, 1)
     rows = amplitudes.shape[0]

time: 355 us -> 348 us (0.980)
  waiting for transfers between devices: 212 us -> 174 us
  blocking collectives: 79.7 us -> 110 us
    all_gather x1 -> x0, waiting for transfers between devices: 37.5 us -> none  [per_device(): whole = lax.all_gather(amplitudes, 'rep', axis=2, tiled=True)]
    all_to_all x0 -> x1, blocking collectives: none -> 30.3 us  [per_device(): blocks = lax.all_to_all(blocks, 'rep', split_axis=0, concat_axis=0)]
    all_gather x1 -> x0, local copies, waits for them, and re-layouts: 4.16 us -> none  [per_device(): whole = lax.all_gather(amplitudes, 'rep', axis=2, tiled=True)]
    unnamed x3 -> x2, waiting for transfers between devices: 134 us -> 133 us
  transfers between devices with their start and end apart: 3 -> 2, of which waited for: 3 -> 2; matrix products, arithmetic and copies ran while one was open for 3% -> 3% of each run, Pallas kernels for 0% -> 0%
where the time goes in v1:
time: 348 us; the launch traced here: 347 us
  waiting for transfers between devices  174 us (50%)
  blocking collectives  110 us (32%)
  matrix products  19.5 us (6%)
  between operations  15.9 us (5%)
  starting transfers between devices  13.7 us (4%)
  local copies, waits for them, and re-layouts  11.9 us (3%)
    unnamed x2, waiting for transfers between devices  133 us
    psum x1, blocking collectives, per_device(): squares = lax.psum(jnp.sum(residual * residual), ('blk', 'rep'))  79.5 us
    all_to_all x1, waiting for transfers between devices, per_device(): lax.all_to_all(whole, 'blk', split_axis=1, concat_axis=0, tiled=True)  40.6 us
    all_to_all x1, blocking collectives, per_device(): blocks = lax.all_to_all(blocks, 'rep', split_axis=0, concat_axis=0)  30.3 us
    all_to_all x1, starting transfers between devices, per_device(): lax.all_to_all(whole, 'blk', split_axis=1, concat_axis=0, tiled=True)  13.6 us
    dot_general x1, matrix products, per_device(): jnp.einsum('aikc,kjbc->iabj', part, crossed, precision=highest)  10.5 us
    dot_general x1, matrix products, per_device(): jnp.einsum('aikc,kjbc->iabj', part, whole, precision=highest)  8.96 us
  transfers between devices with their start and end apart: 2, of which 2 were waited for; matrix products, arithmetic and copies ran while one was open for 3% of the time, Pallas kernels for 0%

profile of v1, /device:TPU:1, one launch (start us, length us, event | category | flops | bytes accessed | tf_op | source)
XLA Modules:
  0.0 347.3 jit_solution(6238439928332378478)
XLA Ops:
  7.2 1.4 stack.2
  8.5 30.3 %all_to_all.14 = f32[4,1,64,4,512]{4,3,2,1,0:T(4,128)S(1)} all-to-all(f32[4,1,64,4,512]{4,3,2,1,0:T(4,128)S(1)} %stack.2), channel_id=1, replica_groups=mesh['blk'=64,'rep'=4] {'rep'}, dimensions={0} | all-to-all | bytes 4194304 | tf_op jit(solution)/shard_map/all_to_all | solution.py:13
  38.8 0.6 copy.11
  39.5 2.5 copy.13
  42.0 0.0 copy-start
  42.0 13.6 %all-to-all-start.1 = ((f32[1,64,16,512]{3,2,0,1:T(8,128)}), f32[1,64,16,512]{3,2,0,1:T(8,128)}, u32[]{:S(2)}, u32[]{:S(2)}) async-start(f32[1,64,16,512]{3,2,0,1:T(8,128)} %copy.13), calls=%async_computation.1 | async-start | bytes 4194304 | tf_op jit(solution)/shard_map/all_to_all | solution.py:15
  55.6 0.0 reduce-scatter.4.cloned.1.call-start
  55.6 0.0 copy-done
  55.7 9.0 %fusion.1 = f32[64,16,8,64]{3,1,2,0:T(8,128)} fusion(f32[64,16,512,1]{2,0,1,3:T(8,128)S(1)} %bitcast.25, f32[8,64,1,512]{3,2,1,0:T(1,128)S(1)} %copy-done), kind=kOutput, calls=%fused_computation.2 | convolution fusion | flops 3221225472 | bytes 5242880 | tf_op jit(solution)/shard_map/aikc,kjbc->iabj/dot_general | solution.py:20
  64.6 40.6 %all-to-all-done.1 = f32[1,64,16,512]{3,2,0,1:T(8,128)} async-done(((f32[1,64,16,512]{3,2,0,1:T(8,128)}), f32[1,64,16,512]{3,2,0,1:T(8,128)}, u32[]{:S(2)}, u32[]{:S(2)}) %all-to-all-start.1) | async-done | bytes 2097184 | tf_op jit(solution)/shard_map/all_to_all | solution.py:15
  105.2 10.5 %add_bitcast_fusion = f32[64,8,16,64]{0,2,1,3:T(8,128)} fusion(f32[64,16,8,64]{3,1,2,0:T(8,128)} %fusion.1, f32[1,64,16,512]{3,2,0,1:T(8,128)} %all-to-all-done.1, f32[8,64,1,512]{3,2,1,0:T(1,128)} %param.8), kind=kOutput, calls=%fused_computation | convolution fusion | flops 3221749760 | bytes 7340032 | tf_op jit(solution)/shard_map/aikc,kjbc->iabj/dot_general | solution.py:27
  115.7 6.1 %copy.14 = f32[64,8,16,64]{3,2,1,0:T(8,128)} copy(f32[64,8,16,64]{0,2,1,3:T(8,128)} %add_bitcast_fusion) | data formatting | bytes 4194304 | tf_op jit(solution)/shard_map/add | solution.py:32
  121.9 0.0 copy-start.3
  121.9 0.0 copy-start.2
  121.9 0.0 copy-start.1
  121.9 0.0 reduce-scatter.4.cloned.1.call-update
  121.9 0.6 copy-done.3
  122.5 0.6 dynamic_slice.6
  123.1 0.0 copy-done.2
  123.1 0.1 dynamic_slice.7
  123.2 0.6 broadcast_add_fusion
  123.8 0.1 broadcast_subtract_fusion
  123.9 133.1 %reduce-scatter.4.cloned.1.call-done = f32[1,8,16,64]{3,2,1,0:T(8,128)} async-done(((f32[64,8,16,64]{3,2,1,0:T(8,128)}), f32[1,8,16,64]{3,2,1,0:T(8,128)}) %reduce-scatter.4.cloned.1.call-update) | async-done | bytes 32784
  257.0 0.0 copy-done.1
  257.0 2.1 multiply_reduce_fusion
  259.1 79.5 %psum.7 = f32[]{:T(128)} all-reduce(f32[]{:T(128)} %get-tuple-element.4), channel_id=1, replica_groups=mesh['blk'=64,'rep'=4] {'blk','rep'}, use_global_device_ids=true, to_apply=%region_3.0 | all-reduce | flops 1 | bytes 8 | tf_op jit(solution)/shard_map/psum | solution.py:43
Async XLA Ops:
  42.0 13.7 %copy-start = (f32[8,64,1,512]{3,2,1,0:T(1,128)S(1)}, f32[8,64,1,512]{3,2,1,0:T(1,128)}, u32[]{:S(2)}) copy-start(f32[8,64,1,512]{3,2,1,0:T(1,128)} %param.7) | copy-start | bytes 3145732
  42.0 63.2 %all-to-all-start.1 = ((f32[1,64,16,512]{3,2,0,1:T(8,128)}), f32[1,64,16,512]{3,2,0,1:T(8,128)}, u32[]{:S(2)}, u32[]{:S(2)}) async-start(f32[1,64,16,512]{3,2,0,1:T(8,128)} %copy.13), calls=%async_computation.1 | async-start | bytes 4194304 | tf_op jit(solution)/shard_map/all_to_all | solution.py:15
  55.6 201.4 %reduce-scatter.4.cloned.1.call-start = ((), (), s32[]{:S(2)}) async-start(), calls=%async_computation.3 | async-start | bytes 4259840
  121.9 0.7 copy-start.3
  121.9 1.2 copy-start.2
  121.9 135.1 %copy-start.1 = (f32[16]{0:T(128)S(1)}, f32[16]{0:T(128)}, u32[]{:S(2)}) copy-start(f32[16]{0:T(128)} %param.11) | copy-start | bytes 196
Sparse Core Ops, SparseCore 0:
  122.0 134.9 reduce-scatter.3
